TPU v7x, 512 devices: a whole 4x4x16 slice. The times are simulated.
512 devices in a mesh: wide: 32 (over x_lo, z), grp: 16 (over y, x_hi, core).
Axes of the slice: x: 4 (x_hi: 2, x_lo: 2; x = x_hi * 2 + x_lo), y: 4, z: 16, core: 2. Of those that a mesh axis runs over, the one named last changes fastest.
Arguments:
- log_hazards: float32 [25, 25], replicated, may hold values from -0.5 to 0.5
- bit_order: int32 [25], replicated, may hold values from 0 to 24, each once
- patients: int32 [256], replicated, may hold values from 0 to 33554431, as said below
- start_dist: float32 [33554432], P(('wide', 'grp')), may hold values from 0.25 to 4
- start_adjoint: float32 [33554432], P(('wide', 'grp')), may hold values from -6 to 6
Outputs:
- distribution: float32 [33554432], P(('wide', 'grp'))
- loglik: float32 [], replicated
- gradient: float32 [25, 25], replicated
- empty_state: float32 [], replicated
Inputs may be any that keep to these rules, and one draw needn't show every extreme that they name: `patients`: each value is a set of events, bit e set when event e is present; every draw has a patient with no event and one with all 25. `bit_order`: A permutation of the events.
All inputs are finite; a program needn't handle non-finite values.
Results may differ from a plain program's by a relative error of at most 0.0003.
Values sent between devices are 32-bit elements; how exact they have to be, the bound alone decides.
A program may use at most 64 MiB of HBM per device.

v0:
```python
import jax
import jax.numpy as jnp
import numpy as np
from jax import lax
from jax.sharding import PartitionSpec as P

highest = lax.Precision.HIGHEST


def partner_2(value, axis, distance):
    mask = 2**distance
    pairs = [(source, source ^ mask) for source in range(lax.axis_size(axis))]
    return lax.ppermute(value, axis, pairs)


def bit_table(number, columns):
    positions = jnp.arange(number, dtype=jnp.int32)
    shifts = jnp.arange(columns, dtype=jnp.int32)
    return (positions[:, None] >> shifts[None, :] & 1).astype(jnp.float32)


def index_bits(position, columns):
    shifts = jnp.arange(columns, dtype=jnp.int32)
    return (position >> shifts & 1).astype(jnp.float32)


def pick_columns(matrix, ranges):
    return jnp.concatenate(
        [matrix[:, begin_at : begin_at + length] for begin_at, length in ranges], axis=1
    )


def order_table(ranges, count_bits):
    listed = [begin_at + offset for begin_at, length in ranges for offset in range(length)]
    table = np.zeros((count_bits, count_bits), np.float32)
    table[np.arange(count_bits), np.array(listed, np.int64)] = 1.0
    return jnp.asarray(table)


def lane_tables(lane_bits_count, lane_count):
    source = jnp.arange(lane_count, dtype=jnp.int32)
    blocks = []
    for lane_bit in range(lane_bits_count):
        stride = 2**lane_bit
        lower_half = source >> lane_bit & 1 == 0
        blocks.append(
            ((source[None, :] == source[:, None] + stride) & lower_half[:, None]).astype(
                jnp.float32
            )
        )
    return jnp.concatenate(blocks, axis=0)


def rate_maker(coupling, diagonal, layout, row_bits, lane_bits):
    row_ranges, lane_ranges, device_ranges, device_values, block_begin, block_count = layout
    block_rows = coupling[block_begin : block_begin + block_count]
    offsets = diagonal[block_begin : block_begin + block_count] + jnp.dot(
        pick_columns(block_rows, device_ranges), device_values, precision=highest
    )
    by_row = jnp.dot(row_bits, pick_columns(block_rows, row_ranges).T, precision=highest)
    by_lane = jnp.dot(lane_bits, pick_columns(block_rows, lane_ranges).T, precision=highest)

    def rate_of(position):
        return jnp.exp(
            offsets[position] + by_row[:, position][:, None] + by_lane[:, position][None, :]
        )

    return rate_of


def row_split(values, row_bit):
    row_count, lane_count = values.shape
    return values.reshape(row_count >> row_bit + 1, 2, 2**row_bit, lane_count)


def join_rows(lower_half, upper_half):
    paired = jnp.stack([lower_half, upper_half], axis=1)
    return paired.reshape(-1, paired.shape[-1])


def local_push(values, rate_of, lane_part, row_start, block_count, lane_push):
    summed = jnp.zeros_like(values)
    if lane_part > 0:
        stacked = jnp.concatenate(
            [rate_of(position) * values for position in range(lane_part)], axis=1
        )
        summed = jnp.dot(stacked, lane_push, precision=highest)
    for position in range(lane_part, block_count):
        moving = row_split(rate_of(position) * values, row_start + position - lane_part)
        summed = summed + join_rows(jnp.zeros_like(moving[:, 0]), moving[:, 0])
    return summed


def local_pull(values, rate_of, lane_part, row_start, block_count, lane_pull):
    summed = jnp.zeros_like(values)
    lane_count = values.shape[1]
    if lane_part > 0:
        partners = jnp.dot(values, lane_pull, precision=highest)
        for position in range(lane_part):
            summed = (
                summed
                + rate_of(position)
                * partners[:, position * lane_count : (position + 1) * lane_count]
            )
    for position in range(lane_part, block_count):
        row_bit = row_start + position - lane_part
        others = row_split(values, row_bit)
        rates = row_split(rate_of(position), row_bit)
        summed = summed + join_rows(rates[:, 0] * others[:, 1], jnp.zeros_like(others[:, 1]))
    return summed


def local_gradient(
    forward, adjoint, rate_of, lane_part, row_start, block_count, lane_pull, lane_low
):
    contribs = []
    lane_count = forward.shape[1]
    if lane_part > 0:
        partners = jnp.dot(adjoint, lane_pull, precision=highest)
        for position in range(lane_part):
            partner = partners[:, position * lane_count : (position + 1) * lane_count]
            contribs.append(
                rate_of(position) * forward * (partner - adjoint) * lane_low[position][None, :]
            )
    for position in range(lane_part, block_count):
        row_bit = row_start + position - lane_part
        others = row_split(adjoint, row_bit)
        rates = row_split(rate_of(position), row_bit)
        forwards = row_split(forward, row_bit)
        lower_term = rates[:, 0] * forwards[:, 0] * (others[:, 1] - others[:, 0])
        contribs.append(join_rows(lower_term, jnp.zeros_like(lower_term)))
    return contribs


def feature_row(contrib, row_bits, lane_bits, device_values, to_global, own_bit):
    per_row = jnp.sum(contrib, axis=1)
    per_lane = jnp.sum(contrib, axis=0)
    whole = jnp.sum(per_row)
    listed = jnp.concatenate(
        [
            jnp.dot(per_row, row_bits, precision=highest),
            jnp.dot(per_lane, lane_bits, precision=highest),
            whole * device_values,
        ]
    )
    own_column = (jnp.arange(to_global.shape[0], dtype=jnp.int32) == own_bit).astype(jnp.float32)
    return jnp.dot(listed, to_global, precision=highest) + whole * own_column


def body(log_hazards, bit_order, patients, start_dist, start_adjoint):
    count_bits = log_hazards.shape[0]
    local_count = start_dist.shape[0]
    patient_count = patients.shape[0]
    wide_count = lax.axis_size("wide")
    grp_count = lax.axis_size("grp")
    wide_bits = wide_count.bit_length() - 1
    grp_bits = grp_count.bit_length() - 1
    local_bits = local_count.bit_length() - 1
    lane_bits_count = min(7, local_bits - wide_bits - grp_bits)
    lane_count = 2**lane_bits_count
    row_count = local_count // lane_count
    row_bits_count = local_bits - lane_bits_count
    wide_index = lax.axis_index("wide")
    grp_index = lax.axis_index("grp")
    wide_values = index_bits(wide_index, wide_bits)
    grp_values = index_bits(grp_index, grp_bits)
    device_values = jnp.concatenate([grp_values, wide_values])
    shifts = jnp.arange(count_bits, dtype=jnp.int32)
    onehot = (bit_order[:, None] == shifts[None, :]).astype(jnp.float32)
    by_bits = jnp.dot(onehot.T, jnp.dot(log_hazards, onehot, precision=highest), precision=highest)
    diagonal = jnp.diagonal(by_bits)
    coupling = by_bits * (1.0 - jnp.eye(count_bits, dtype=jnp.float32))
    row_bits = bit_table(row_count, row_bits_count)
    lane_bits = bit_table(lane_count, lane_bits_count)
    lane_push = lane_tables(lane_bits_count, lane_count)
    lane_pull = lane_push.T
    lane_low = 1.0 - lane_bits.T
    home_rows = [(lane_bits_count, row_bits_count)]
    lane_ranges = [(0, lane_bits_count)]
    home_devices = [(local_bits, grp_bits), (local_bits + grp_bits, wide_bits)]
    home_rate = rate_maker(
        coupling,
        diagonal,
        (home_rows, lane_ranges, home_devices, device_values, 0, count_bits),
        row_bits,
        lane_bits,
    )
    home_global = order_table(home_rows + lane_ranges + home_devices, count_bits)
    away_rows = [(lane_bits_count, row_bits_count - grp_bits), (local_bits, grp_bits)]
    away_devices = [(local_bits - grp_bits, grp_bits), (local_bits + grp_bits, wide_bits)]
    away_rate = rate_maker(
        coupling,
        diagonal,
        (away_rows, lane_ranges, away_devices, device_values, local_bits, grp_bits),
        row_bits,
        lane_bits,
    )
    away_global = order_table(away_rows + lane_ranges + away_devices, count_bits)
    row_start = row_bits_count - grp_bits

    def regroup(values):
        three_way = values.reshape(grp_count, -1, lane_count)
        arrived = lax.all_to_all(three_way, "grp", split_axis=0, concat_axis=0, tiled=True)
        return arrived.reshape(row_count, lane_count)

    def wide_swap(values, wide_bit):
        return partner_2(values, "wide", wide_bit)

    denominator = jnp.ones((row_count, lane_count), jnp.float32)
    for position in range(lane_bits_count):
        denominator = denominator + home_rate(position) * lane_low[position][None, :]
    for position in range(lane_bits_count, local_bits):
        rates = row_split(home_rate(position), position - lane_bits_count)
        denominator = denominator + join_rows(rates[:, 0], jnp.zeros_like(rates[:, 0]))
    for grp_bit in range(grp_bits):
        denominator = denominator + home_rate(local_bits + grp_bit) * (1.0 - grp_values[grp_bit])
    for wide_bit in range(wide_bits):
        denominator = denominator + home_rate(local_bits + grp_bits + wide_bit) * (
            1.0 - wide_values[wide_bit]
        )
    row_iota = lax.broadcasted_iota(jnp.int32, (row_count, lane_count), 0)
    lane_iota = lax.broadcasted_iota(jnp.int32, (row_count, lane_count), 1)
    first_device = (wide_index == 0) & (grp_index == 0)
    first_state = first_device & (row_iota == 0) & (lane_iota == 0)
    source = jnp.where(first_state, float(2**count_bits), 0.0).astype(jnp.float32)
    forward = start_dist.reshape(row_count, lane_count)
    summed = source + local_push(forward, home_rate, lane_bits_count, 0, local_bits, lane_push)
    away = regroup(forward)
    summed = summed + regroup(local_push(away, away_rate, 0, row_start, grp_bits, lane_push))
    for wide_bit in range(wide_bits):
        received = wide_swap(home_rate(local_bits + grp_bits + wide_bit) * forward, wide_bit)
        summed = summed + wide_values[wide_bit] * received
    forward = summed / denominator
    present = patients[:, None] >> shifts[None, :] & 1
    state_index = jnp.sum(present << bit_order[None, :], axis=1)
    device_number = wide_index * grp_count + grp_index
    on_device = state_index >> local_bits == device_number
    local_index = jnp.where(on_device, state_index & local_count - 1, local_count)
    counts = (
        jnp.zeros((local_count,), jnp.float32)
        .at[local_index]
        .add(1.0, mode="drop")
        .reshape(row_count, lane_count)
    )
    flattened = forward.reshape(-1)
    picked = flattened[jnp.where(on_device, local_index, 0)]
    log_sum = jnp.sum(jnp.where(on_device, jnp.log(picked), 0.0))
    log_first = jnp.where(first_device, jnp.log(flattened[0]), 0.0)
    weights = counts / (patient_count * forward)
    adjoint = start_adjoint.reshape(row_count, lane_count) * 2.0 ** (-(count_bits // 2))
    summed = weights + local_pull(adjoint, home_rate, lane_bits_count, 0, local_bits, lane_pull)
    away = regroup(adjoint)
    summed = summed + regroup(local_pull(away, away_rate, 0, row_start, grp_bits, lane_pull))
    for wide_bit in range(wide_bits):
        received = wide_swap(adjoint, wide_bit)
        summed = (
            summed
            + (1.0 - wide_values[wide_bit]) * home_rate(local_bits + grp_bits + wide_bit) * received
        )
    adjoint = summed / denominator
    grad_rows = []
    home_terms = local_gradient(
        forward, adjoint, home_rate, lane_bits_count, 0, local_bits, lane_pull, lane_low
    )
    for position in range(local_bits):
        grad_rows.append(
            feature_row(
                home_terms[position], row_bits, lane_bits, device_values, home_global, position
            )
        )
    three_way = (grp_count, -1, lane_count)
    arrived = (
        lax.all_to_all(forward.reshape(three_way), "grp", split_axis=0, concat_axis=0, tiled=True),
        lax.all_to_all(adjoint.reshape(three_way), "grp", split_axis=0, concat_axis=0, tiled=True),
    )
    away_forward = arrived[0].reshape(row_count, lane_count)
    away_adjoint = arrived[1].reshape(row_count, lane_count)
    away_terms = local_gradient(
        away_forward, away_adjoint, away_rate, 0, row_start, grp_bits, lane_pull, lane_low
    )
    for position in range(grp_bits):
        grad_rows.append(
            feature_row(
                away_terms[position],
                row_bits,
                lane_bits,
                device_values,
                away_global,
                local_bits + position,
            )
        )
    for wide_bit in range(wide_bits):
        global_bit = local_bits + grp_bits + wide_bit
        received = wide_swap(adjoint, wide_bit)
        contrib = (
            (1.0 - wide_values[wide_bit]) * home_rate(global_bit) * forward * (received - adjoint)
        )
        grad_rows.append(
            feature_row(contrib, row_bits, lane_bits, device_values, home_global, global_bit)
        )
    partial_grad = jnp.stack(grad_rows)
    grad_total, log_total, empty_state = lax.psum(
        (partial_grad, log_sum, log_first), ("wide", "grp")
    )
    gradient = jnp.dot(onehot, jnp.dot(grad_total, onehot.T, precision=highest), precision=highest)
    loglik = log_total / patient_count
    distribution = jnp.where(first_state, 0.0, forward)
    return (distribution.reshape(-1), loglik, gradient, empty_state)


def solution(mesh):
    return jax.shard_map(
        body,
        mesh=mesh,
        in_specs=(P(), P(), P(), P(("wide", "grp")), P(("wide", "grp"))),
        out_specs=(P(("wide", "grp")), P(), P(), P()),
        check_vma=False,
    )
```

profile of v0, /device:TPU:1, one launch (start us, length us, event | category | flops | bytes accessed | tf_op | source)
XLA Modules:
  0.0 466.9 jit_solution(10316019383893845244)
XLA Ops:
  7.5 6.0 %fusion.490 = (f32[512]{0:T(512)S(1)}, f32[512,1]{0,1:T(1,128)}, f32[512,1]{0,1:T(1,128)S(1)}, f32[512,1]{0,1:T(1,128)S(1)}, f32[512,1]{0,1:T(1,128)S(1)}, /*ind...) fusion(f32[]{:T(128)} %broadcast.1002, f32[512,25]{0,1:T(8,128)S(1)} %fusion.133, ...), kind=kLoop, calls=%fused_computation.907 | loop fusion | flops 4096 | bytes 34852 | tf_op jit(solution)/shard_map/add | solution.py:65
  20.2 6.1 %slice_add_fusion.3 = (f32[512,1]{0,1:T(1,128)}, f32[512,1]{0,1:T(1,128)}, f32[512,1]{0,1:T(1,128)}, f32[512,1]{0,1:T(1,128)}, f32[512,1]{0,1:T(1,128)S(1)}, /*i...) fusion(f32[512,25]{0,1:T(8,128)S(1)} %fusion.133, f32[]{:T(128)} %bitcast.119, ...), kind=kLoop, calls=%fused_computation.517 | loop fusion | flops 4608 | bytes 36900 | tf_op jit(solution)/shard_map/add | solution.py:65
  26.5 2.5 fusion.100
  29.1 4.4 collective-permute-start
  33.4 4.9 %collective-permute-start.1 = (f32[512,128]{1,0:T(8,128)}, f32[512,128]{1,0:T(8,128)}, u32[]{:S(2)}, u32[]{:S(2)}) collective-permute-start(f32[512,128]{1,0:T(8,128)} %get-tuple-element.143), channel_id=1, source_target_pairs={{0,32},{16,48},{32,0},{48,16},{64,96},{80,112},{96,64},{112,80},{1... | collective-permute-start | bytes 786440 | tf_op jit(solution)/shard_map/ppermute | solution.py:13
  38.3 8.8 %collective-permute-start.2 = (f32[512,128]{1,0:T(8,128)}, f32[512,128]{1,0:T(8,128)}, u32[]{:S(2)}, u32[]{:S(2)}) collective-permute-start(f32[512,128]{1,0:T(8,128)} %get-tuple-element.144), channel_id=1, source_target_pairs={{0,64},{16,80},{32,96},{48,112},{64,0},{80,16},{96,32},{112,48},{1... | collective-permute-start | bytes 786440 | tf_op jit(solution)/shard_map/ppermute | solution.py:13
  47.2 7.9 %collective-permute-start.3 = (f32[512,128]{1,0:T(8,128)}, f32[512,128]{1,0:T(8,128)}, u32[]{:S(2)}, u32[]{:S(2)}) collective-permute-start(f32[512,128]{1,0:T(8,128)} %get-tuple-element.145), channel_id=1, source_target_pairs={{0,128},{16,144},{32,160},{48,176},{64,192},{80,208},{96,224},{112... | collective-permute-start | bytes 786440 | tf_op jit(solution)/shard_map/ppermute | solution.py:13
  55.1 3.1 collective-permute-start.4
  59.1 8.7 %all-to-all-start.2 = ((f32[16,32,128]{2,1,0:T(8,128)}), f32[16,32,128]{2,1,0:T(8,128)S(1)}, u32[]{:S(2)}, u32[]{:S(2)}) async-start(f32[16,32,128]{2,1,0:T(8,128)} %bitcast.160), calls=%async_computation.2 | async-start | bytes 524288 | tf_op jit(solution)/shard_map/all_to_all | solution.py:203
  71.5 3.1 fusion.264
  77.0 6.2 %fusion.483 = (f32[512]{0:T(512)S(1)}, f32[512,1]{0,1:T(1,128)}, f32[512,1]{0,1:T(1,128)}, f32[512]{0:T(512)S(1)}, f32[512,1]{0,1:T(1,128)}, /*index=5*/f32[512]...) fusion(f32[]{:T(128)} %broadcast.1002, ...), kind=kLoop, calls=%fused_computation.900 | loop fusion | flops 4096 | bytes 47140 | tf_op jit(solution)/shard_map/add | solution.py:65
  96.2 1.8 slice_multiply_fusion.25
  98.0 1.8 slice_multiply_fusion.31
  101.5 1.7 slice_multiply_fusion.28
  106.6 1.7 slice_multiply_fusion.30
  110.6 7.2 %all-to-all-start = ((f32[16,32,128]{2,1,0:T(8,128)}), f32[16,32,128]{2,1,0:T(8,128)S(1)}, u32[]{:S(2)}, u32[]{:S(2)}) async-start(f32[16,32,128]{2,1,0:T(8,128)} %bitcast.66), calls=%async_computation | async-start | bytes 524288 | tf_op jit(solution)/shard_map/all_to_all | solution.py:203
  117.8 2.1 slice_multiply_fusion.32
  119.9 6.6 %all-to-all-done = f32[16,32,128]{2,1,0:T(8,128)S(1)} async-done(((f32[16,32,128]{2,1,0:T(8,128)}), f32[16,32,128]{2,1,0:T(8,128)S(1)}, u32[]{:S(2)}, u32[]{:S(2)}) %all-to-all-start) | async-done | bytes 262176 | tf_op jit(solution)/shard_map/all_to_all | solution.py:203
  130.1 4.8 %all-to-all-start.3 = ((f32[16,32,128]{2,1,0:T(8,128)}), f32[16,32,128]{2,1,0:T(8,128)}, u32[]{:S(2)}, u32[]{:S(2)}) async-start(f32[16,32,128]{2,1,0:T(8,128)} %fusion.91), calls=%async_computation.3 | async-start | bytes 524288 | tf_op jit(solution)/shard_map/all_to_all | solution.py:203
  138.7 2.6 collective-permute-start.5
  141.3 3.1 collective-permute-start.6
  144.4 5.2 %collective-permute-start.7 = (f32[512,128]{1,0:T(8,128)}, f32[512,128]{1,0:T(8,128)}, u32[]{:S(2)}, u32[]{:S(2)}) collective-permute-start(f32[512,128]{1,0:T(8,128)} %get-tuple-element.113), channel_id=1, source_target_pairs={{0,64},{16,80},{32,96},{48,112},{64,0},{80,16},{96,32},{112,48},{1... | collective-permute-start | bytes 786440 | tf_op jit(solution)/shard_map/ppermute | solution.py:13
  149.6 1.9 collective-permute-start.8
  151.6 1.9 collective-permute-start.9
  153.5 9.0 %all-to-all-start.1 = ((f32[16,32,128]{2,1,0:T(8,128)}), f32[16,32,128]{2,1,0:T(8,128)}, u32[]{:S(2)}, u32[]{:S(2)}) async-start(f32[16,32,128]{2,1,0:T(8,128)} %fusion.93), calls=%async_computation.1 | async-start | bytes 524288 | tf_op jit(solution)/shard_map/all_to_all | solution.py:203
  164.4 1.7 stack.270
  167.0 1.8 stack.248
  200.4 2.7 scatter_custom_fusion
  204.8 10.6 %fusion.84 = (f32[512,128]{1,0:T(8,128)}, f32[512,128]{1,0:T(8,128)}) fusion(f32[512,128]{1,0:T(8,128)} %bitcast.870, f32[512,128]{1,0:T(8,128)} %bitcast.863, f32[512,128]{1,0:T(8,128)} %bitcast.862, f32[512,896]{1,0:T(8,128)S(1)} %fusion.414, f32[16,32,128]{2,1,0:T(8,128)} %all-to-all-done.3, f32[1,2,256,128]{3,2,1,0:T(8,128)} %stack.278, ...), kind=kOutput, calls=%fused_computation.214 | convolution fusion | flops 713555968 | bytes 12508344 | tf_op jit(solution)/shard_map/dot_general | solution.py:87
  215.5 3.2 collective-permute-start.11
  218.7 7.5 %collective-permute-start.12 = (f32[512,128]{1,0:T(8,128)}, f32[512,128]{1,0:T(8,128)}, u32[]{:S(2)}, u32[]{:S(2)}) collective-permute-start(f32[512,128]{1,0:T(8,128)} %get-tuple-element.284), channel_id=1, source_target_pairs={{0,64},{16,80},{32,96},{48,112},{64,0},{80,16},{96,32},{112,48},{1... | collective-permute-start | bytes 786440 | tf_op jit(solution)/shard_map/ppermute | solution.py:13
  226.3 8.8 %collective-permute-start.13 = (f32[512,128]{1,0:T(8,128)}, f32[512,128]{1,0:T(8,128)}, u32[]{:S(2)}, u32[]{:S(2)}) collective-permute-start(f32[512,128]{1,0:T(8,128)} %get-tuple-element.284), channel_id=1, source_target_pairs={{0,128},{16,144},{32,160},{48,176},{64,192},{80,208},{96,224},{112... | collective-permute-start | bytes 786440 | tf_op jit(solution)/shard_map/ppermute | solution.py:13
  235.1 2.2 collective-permute-start.14
  237.3 1.9 fusion.498
  239.2 2.8 collective-permute-start.10
  252.1 9.2 %all-to-all-start.4 = ((f32[16,32,128]{2,1,0:T(8,128)}), f32[16,32,128]{2,1,0:T(8,128)S(1)}, u32[]{:S(2)}, u32[]{:S(2)}) async-start(f32[16,32,128]{2,1,0:T(8,128)} %bitcast.293), calls=%async_computation.4 | async-start | bytes 524288 | tf_op jit(solution)/shard_map/all_to_all | solution.py:273
  261.4 2.4 fusion.54
  277.9 1.9 fusion.477
  283.1 1.8 fusion.141
  285.6 2.9 gather_fusion.1
  290.2 7.2 %all-to-all-start.5 = ((f32[16,32,128]{2,1,0:T(8,128)}), f32[16,32,128]{2,1,0:T(8,128)S(1)}, u32[]{:S(2)}, u32[]{:S(2)}) async-start(f32[16,32,128]{2,1,0:T(8,128)} %bitcast.295), calls=%async_computation.5 | async-start | bytes 524288 | tf_op jit(solution)/shard_map/all_to_all | solution.py:274
  300.6 1.8 fusion.139
  302.4 3.7 all-to-all-done.5
  306.1 1.8 pad_reduce_fusion.2
  326.6 11.2 %broadcast_multiply_fusion.1 = (f32[9]{0:T(128)S(1)}, f32[9]{0:T(128)S(1)}, f32[9]{0:T(128)S(1)}, f32[9]{0:T(128)S(1)}, f32[9]{0:T(128)S(1)}, /*index=5*/f32[9]{...) fusion(f32[]{:T(128)} %get-tuple-element.5, ...), kind=kLoop, calls=%fused_computation.779 | loop fusion | flops 171 | bytes 756 | tf_op jit(solution)/shard_map/mul | solution.py:143
  352.8 4.5 broadcast_multiply_fusion.19
  363.3 1.8 fusion.52
  365.1 98.9 %all-reduce.39 = (f32[]{:T(128)}, f32[25,25]{1,0:T(8,128)S(1)}, f32[]{:T(128)}) all-reduce(f32[]{:T(128)} %select_reduce_fusion, f32[25,25]{1,0:T(8,128)S(1)} %stack.321, f32[]{:T(128)S(6)} %select_n.72), channel_id=1, replica_groups=mesh['wide'=32,'grp'=16] {'wide','grp'}, use_global_device_ids=true, to_apply=%region_2.3 | all-reduce | flops 627 | bytes 5016 | tf_op jit(solution)/shard_map/psum | solution.py:302
  (542 shorter events, 150.1 us)
Async XLA Ops:
  0.7 69.5 %copy-start.43 = (f32[5]{0:T(128)}, f32[5]{0:T(128)S(1)}, u32[]{:S(2)}) copy-start(f32[5]{0:T(128)S(1)} %and_convert_fusion) | copy-start | bytes 64
  1.4 68.9 %copy-start.46 = (f32[4]{0:T(128)}, f32[4]{0:T(128)S(1)}, u32[]{:S(2)}) copy-start(f32[4]{0:T(128)S(1)} %and_convert_fusion.1) | copy-start | bytes 52
  16.9 41.4 %copy-start.2 = (f32[65536]{0:T(1024)S(1)}, f32[65536]{0:T(1024)}, u32[]{:S(2)}) copy-start(f32[65536]{0:T(1024)} %param.11) | copy-start | bytes 786436
  26.4 57.0 %copy-start.62 = (f32[512,1]{0,1:T(1,128)}, f32[512,1]{0,1:T(1,128)S(1)}, u32[]{:S(2)}) copy-start(f32[512,1]{0,1:T(1,128)S(1)} %get-tuple-element.155) | copy-start | bytes 6148
  26.4 57.0 %copy-start.64 = (f32[512,1]{0,1:T(1,128)}, f32[512,1]{0,1:T(1,128)S(1)}, u32[]{:S(2)}) copy-start(f32[512,1]{0,1:T(1,128)S(1)} %get-tuple-element.151) | copy-start | bytes 6148
  26.4 57.0 %copy-start.66 = (f32[512,1]{0,1:T(1,128)}, f32[512,1]{0,1:T(1,128)S(1)}, u32[]{:S(2)}) copy-start(f32[512,1]{0,1:T(1,128)S(1)} %get-tuple-element.152) | copy-start | bytes 6148
  26.4 57.0 %copy-start.68 = (f32[512,1]{0,1:T(1,128)}, f32[512,1]{0,1:T(1,128)S(1)}, u32[]{:S(2)}) copy-start(f32[512,1]{0,1:T(1,128)S(1)} %get-tuple-element.153) | copy-start | bytes 6148
  26.4 57.0 %copy-start.70 = (f32[512,1]{0,1:T(1,128)}, f32[512,1]{0,1:T(1,128)S(1)}, u32[]{:S(2)}) copy-start(f32[512,1]{0,1:T(1,128)S(1)} %get-tuple-element.154) | copy-start | bytes 6148
  26.4 60.7 %copy-start.115 = (s32[256]{0:T(256)S(1)}, s32[256]{0:T(256)}, u32[]{:S(2)}) copy-start(s32[256]{0:T(256)} %param.9) | copy-start | bytes 3076
  26.4 60.7 %copy-start.116 = (s32[25]{0:T(128)S(1)}, s32[25]{0:T(128)}, u32[]{:S(2)}) copy-start(s32[25]{0:T(128)} %param.8) | copy-start | bytes 304
  29.0 59.5 %copy-start.40 = (f32[512,896]{1,0:T(8,128)}, f32[512,896]{1,0:T(8,128)S(1)}, u32[]{:S(2)}) copy-start(f32[512,896]{1,0:T(8,128)S(1)} %get-tuple-element.141) | copy-start | bytes 5505028
  29.1 109.6 %collective-permute-start = (f32[512,128]{1,0:T(8,128)}, f32[512,128]{1,0:T(8,128)}, u32[]{:S(2)}, u32[]{:S(2)}) collective-permute-start(f32[512,128]{1,0:T(8,128)} %get-tuple-element.142), channel_id=1, source_target_pairs={{0,16},{16,0},{32,48},{48,32},{64,80},{80,64},{96,112},{112,96},{1... | collective-permute-start | bytes 786440 | tf_op jit(solution)/shard_map/ppermute | solution.py:13
  33.4 107.9 %collective-permute-start.1 = (f32[512,128]{1,0:T(8,128)}, f32[512,128]{1,0:T(8,128)}, u32[]{:S(2)}, u32[]{:S(2)}) collective-permute-start(f32[512,128]{1,0:T(8,128)} %get-tuple-element.143), channel_id=1, source_target_pairs={{0,32},{16,48},{32,0},{48,16},{64,96},{80,112},{96,64},{112,80},{1... | collective-permute-start | bytes 786440 | tf_op jit(solution)/shard_map/ppermute | solution.py:13
  38.3 106.1 %collective-permute-start.2 = (f32[512,128]{1,0:T(8,128)}, f32[512,128]{1,0:T(8,128)}, u32[]{:S(2)}, u32[]{:S(2)}) collective-permute-start(f32[512,128]{1,0:T(8,128)} %get-tuple-element.144), channel_id=1, source_target_pairs={{0,64},{16,80},{32,96},{48,112},{64,0},{80,16},{96,32},{112,48},{1... | collective-permute-start | bytes 786440 | tf_op jit(solution)/shard_map/ppermute | solution.py:13
  47.2 102.5 %collective-permute-start.3 = (f32[512,128]{1,0:T(8,128)}, f32[512,128]{1,0:T(8,128)}, u32[]{:S(2)}, u32[]{:S(2)}) collective-permute-start(f32[512,128]{1,0:T(8,128)} %get-tuple-element.145), channel_id=1, source_target_pairs={{0,128},{16,144},{32,160},{48,176},{64,192},{80,208},{96,224},{112... | collective-permute-start | bytes 786440 | tf_op jit(solution)/shard_map/ppermute | solution.py:13
  55.1 96.5 %collective-permute-start.4 = (f32[512,128]{1,0:T(8,128)}, f32[512,128]{1,0:T(8,128)}, u32[]{:S(2)}, u32[]{:S(2)}) collective-permute-start(f32[512,128]{1,0:T(8,128)} %get-tuple-element.146), channel_id=1, source_target_pairs={{0,256},{16,272},{32,288},{48,304},{64,320},{80,336},{96,352},{112... | collective-permute-start | bytes 786440 | tf_op jit(solution)/shard_map/ppermute | solution.py:13
  59.1 51.5 %all-to-all-start.2 = ((f32[16,32,128]{2,1,0:T(8,128)}), f32[16,32,128]{2,1,0:T(8,128)S(1)}, u32[]{:S(2)}, u32[]{:S(2)}) async-start(f32[16,32,128]{2,1,0:T(8,128)} %bitcast.160), calls=%async_computation.2 | async-start | bytes 524288 | tf_op jit(solution)/shard_map/all_to_all | solution.py:203
  110.6 15.9 %all-to-all-start = ((f32[16,32,128]{2,1,0:T(8,128)}), f32[16,32,128]{2,1,0:T(8,128)S(1)}, u32[]{:S(2)}, u32[]{:S(2)}) async-start(f32[16,32,128]{2,1,0:T(8,128)} %bitcast.66), calls=%async_computation | async-start | bytes 524288 | tf_op jit(solution)/shard_map/all_to_all | solution.py:203
  130.1 23.4 %all-to-all-start.3 = ((f32[16,32,128]{2,1,0:T(8,128)}), f32[16,32,128]{2,1,0:T(8,128)}, u32[]{:S(2)}, u32[]{:S(2)}) async-start(f32[16,32,128]{2,1,0:T(8,128)} %fusion.91), calls=%async_computation.3 | async-start | bytes 524288 | tf_op jit(solution)/shard_map/all_to_all | solution.py:203
  136.9 29.3 %copy-start.30 = (f32[128,1,2,128]{3,2,1,0:T(2,128)S(1)}, f32[128,1,2,128]{3,2,1,0:T(2,128)}, u32[]{:S(2)}) copy-start(f32[128,1,2,128]{3,2,1,0:T(2,128)} %get-tuple-element.137) | copy-start | bytes 393220
  137.9 30.8 %copy-start.29 = (f32[128,1,2,128]{3,2,1,0:T(2,128)S(1)}, f32[128,1,2,128]{3,2,1,0:T(2,128)}, u32[]{:S(2)}) copy-start(f32[128,1,2,128]{3,2,1,0:T(2,128)} %get-tuple-element.138) | copy-start | bytes 393220
  138.7 66.0 %collective-permute-start.5 = (f32[512,128]{1,0:T(8,128)}, f32[512,128]{1,0:T(8,128)}, u32[]{:S(2)}, u32[]{:S(2)}) collective-permute-start(f32[512,128]{1,0:T(8,128)} %get-tuple-element.113), channel_id=1, source_target_pairs={{0,16},{16,0},{32,48},{48,32},{64,80},{80,64},{96,112},{112,96},{1... | collective-permute-start | bytes 786440 | tf_op jit(solution)/shard_map/ppermute | solution.py:13
  141.3 63.4 %collective-permute-start.6 = (f32[512,128]{1,0:T(8,128)}, f32[512,128]{1,0:T(8,128)}, u32[]{:S(2)}, u32[]{:S(2)}) collective-permute-start(f32[512,128]{1,0:T(8,128)} %get-tuple-element.113), channel_id=1, source_target_pairs={{0,32},{16,48},{32,0},{48,16},{64,96},{80,112},{96,64},{112,80},{1... | collective-permute-start | bytes 786440 | tf_op jit(solution)/shard_map/ppermute | solution.py:13
  144.4 60.3 %collective-permute-start.7 = (f32[512,128]{1,0:T(8,128)}, f32[512,128]{1,0:T(8,128)}, u32[]{:S(2)}, u32[]{:S(2)}) collective-permute-start(f32[512,128]{1,0:T(8,128)} %get-tuple-element.113), channel_id=1, source_target_pairs={{0,64},{16,80},{32,96},{48,112},{64,0},{80,16},{96,32},{112,48},{1... | collective-permute-start | bytes 786440 | tf_op jit(solution)/shard_map/ppermute | solution.py:13
  149.6 55.1 %collective-permute-start.8 = (f32[512,128]{1,0:T(8,128)}, f32[512,128]{1,0:T(8,128)}, u32[]{:S(2)}, u32[]{:S(2)}) collective-permute-start(f32[512,128]{1,0:T(8,128)} %get-tuple-element.113), channel_id=1, source_target_pairs={{0,128},{16,144},{32,160},{48,176},{64,192},{80,208},{96,224},{112... | collective-permute-start | bytes 786440 | tf_op jit(solution)/shard_map/ppermute | solution.py:13
  151.6 53.2 %collective-permute-start.9 = (f32[512,128]{1,0:T(8,128)}, f32[512,128]{1,0:T(8,128)}, u32[]{:S(2)}, u32[]{:S(2)}) collective-permute-start(f32[512,128]{1,0:T(8,128)} %get-tuple-element.113), channel_id=1, source_target_pairs={{0,256},{16,272},{32,288},{48,304},{64,320},{80,336},{96,352},{112... | collective-permute-start | bytes 786440 | tf_op jit(solution)/shard_map/ppermute | solution.py:13
  153.5 51.3 %all-to-all-start.1 = ((f32[16,32,128]{2,1,0:T(8,128)}), f32[16,32,128]{2,1,0:T(8,128)}, u32[]{:S(2)}, u32[]{:S(2)}) async-start(f32[16,32,128]{2,1,0:T(8,128)} %fusion.93), calls=%async_computation.1 | async-start | bytes 524288 | tf_op jit(solution)/shard_map/all_to_all | solution.py:203
  215.5 28.9 %copy-start.16 = (f32[128,2,2,128]{3,2,1,0:T(2,128)S(1)}, f32[128,2,2,128]{3,2,1,0:T(2,128)}, u32[]{:S(2)}) copy-start(f32[128,2,2,128]{3,2,1,0:T(2,128)} %copy-done.15) | copy-start | bytes 786436
  215.5 99.1 %collective-permute-start.11 = (f32[512,128]{1,0:T(8,128)}, f32[512,128]{1,0:T(8,128)}, u32[]{:S(2)}, u32[]{:S(2)}) collective-permute-start(f32[512,128]{1,0:T(8,128)} %get-tuple-element.284), channel_id=1, source_target_pairs={{0,32},{16,48},{32,0},{48,16},{64,96},{80,112},{96,64},{112,80},{1... | collective-permute-start | bytes 786440 | tf_op jit(solution)/shard_map/ppermute | solution.py:13
  218.7 95.8 %collective-permute-start.12 = (f32[512,128]{1,0:T(8,128)}, f32[512,128]{1,0:T(8,128)}, u32[]{:S(2)}, u32[]{:S(2)}) collective-permute-start(f32[512,128]{1,0:T(8,128)} %get-tuple-element.284), channel_id=1, source_target_pairs={{0,64},{16,80},{32,96},{48,112},{64,0},{80,16},{96,32},{112,48},{1... | collective-permute-start | bytes 786440 | tf_op jit(solution)/shard_map/ppermute | solution.py:13
  226.3 88.3 %collective-permute-start.13 = (f32[512,128]{1,0:T(8,128)}, f32[512,128]{1,0:T(8,128)}, u32[]{:S(2)}, u32[]{:S(2)}) collective-permute-start(f32[512,128]{1,0:T(8,128)} %get-tuple-element.284), channel_id=1, source_target_pairs={{0,128},{16,144},{32,160},{48,176},{64,192},{80,208},{96,224},{112... | collective-permute-start | bytes 786440 | tf_op jit(solution)/shard_map/ppermute | solution.py:13
  235.1 79.5 %collective-permute-start.14 = (f32[512,128]{1,0:T(8,128)}, f32[512,128]{1,0:T(8,128)}, u32[]{:S(2)}, u32[]{:S(2)}) collective-permute-start(f32[512,128]{1,0:T(8,128)} %get-tuple-element.284), channel_id=1, source_target_pairs={{0,256},{16,272},{32,288},{48,304},{64,320},{80,336},{96,352},{112... | collective-permute-start | bytes 786440 | tf_op jit(solution)/shard_map/ppermute | solution.py:13
  239.2 80.5 %collective-permute-start.10 = (f32[512,128]{1,0:T(8,128)}, f32[512,128]{1,0:T(8,128)}, u32[]{:S(2)}, u32[]{:S(2)}) collective-permute-start(f32[512,128]{1,0:T(8,128)} %get-tuple-element.284), channel_id=1, source_target_pairs={{0,16},{16,0},{32,48},{48,32},{64,80},{80,64},{96,112},{112,96},{1... | collective-permute-start | bytes 786440 | tf_op jit(solution)/shard_map/ppermute | solution.py:13
  252.1 38.1 %all-to-all-start.4 = ((f32[16,32,128]{2,1,0:T(8,128)}), f32[16,32,128]{2,1,0:T(8,128)S(1)}, u32[]{:S(2)}, u32[]{:S(2)}) async-start(f32[16,32,128]{2,1,0:T(8,128)} %bitcast.293), calls=%async_computation.4 | async-start | bytes 524288 | tf_op jit(solution)/shard_map/all_to_all | solution.py:273
  290.2 15.9 %all-to-all-start.5 = ((f32[16,32,128]{2,1,0:T(8,128)}), f32[16,32,128]{2,1,0:T(8,128)S(1)}, u32[]{:S(2)}, u32[]{:S(2)}) async-start(f32[16,32,128]{2,1,0:T(8,128)} %bitcast.295), calls=%async_computation.5 | async-start | bytes 524288 | tf_op jit(solution)/shard_map/all_to_all | solution.py:274
  321.4 28.8 %copy-start.126 = (f32[9]{0:T(128)S(1)}, f32[9]{0:T(128)}, u32[]{:S(2)}) copy-start(f32[9]{0:T(128)} %convolution_bitcast_fusion.15) | copy-start | bytes 112
  321.4 28.8 %copy-start.127 = (f32[7]{0:T(128)S(1)}, f32[7]{0:T(128)}, u32[]{:S(2)}) copy-start(f32[7]{0:T(128)} %convolution_bitcast_fusion.56) | copy-start | bytes 88
  321.4 29.6 %copy-start.128 = (f32[9]{0:T(128)S(1)}, f32[9]{0:T(128)}, u32[]{:S(2)}) copy-start(f32[9]{0:T(128)} %convolution_bitcast_fusion.16) | copy-start | bytes 112
  321.4 29.6 %copy-start.130 = (f32[7]{0:T(128)S(1)}, f32[7]{0:T(128)}, u32[]{:S(2)}) copy-start(f32[7]{0:T(128)} %convolution_bitcast_fusion.58) | copy-start | bytes 88
  321.4 30.5 %copy-start.129 = (f32[9]{0:T(128)S(1)}, f32[9]{0:T(128)}, u32[]{:S(2)}) copy-start(f32[9]{0:T(128)} %convolution_bitcast_fusion.17) | copy-start | bytes 112
  321.4 30.5 %copy-start.131 = (f32[7]{0:T(128)S(1)}, f32[7]{0:T(128)}, u32[]{:S(2)}) copy-start(f32[7]{0:T(128)} %convolution_bitcast_fusion.60) | copy-start | bytes 88
  321.4 36.7 %copy-start.119 = (f32[9]{0:T(128)S(1)}, f32[9]{0:T(128)}, u32[]{:S(2)}) copy-start(f32[9]{0:T(128)} %convolution_bitcast_fusion.19) | copy-start | bytes 112
  321.5 36.7 %copy-start.120 = (f32[7]{0:T(128)S(1)}, f32[7]{0:T(128)}, u32[]{:S(2)}) copy-start(f32[7]{0:T(128)} %convolution_bitcast_fusion.64) | copy-start | bytes 88
  321.5 37.5 %copy-start.118 = (f32[9]{0:T(128)S(1)}, f32[9]{0:T(128)}, u32[]{:S(2)}) copy-start(f32[9]{0:T(128)} %convolution_bitcast_fusion.20) | copy-start | bytes 112
  321.5 37.5 %copy-start.121 = (f32[7]{0:T(128)S(1)}, f32[7]{0:T(128)}, u32[]{:S(2)}) copy-start(f32[7]{0:T(128)} %convolution_bitcast_fusion.66) | copy-start | bytes 88
  321.5 41.8 %copy-start.132 = (pred[128]{0:T(512)(128)(4,1)S(1)}, pred[128]{0:T(512)(128)(4,1)}, u32[]{:S(2)}) copy-start(pred[128]{0:T(512)(128)(4,1)} %iota_compare_fusion.12) | copy-start | bytes 388
  321.5 41.8 %copy-start.133 = (pred[512]{0:T(512)(128)(4,1)S(1)}, pred[512]{0:T(512)(128)(4,1)}, u32[]{:S(2)}) copy-start(pred[512]{0:T(512)(128)(4,1)} %fusion.269) | copy-start | bytes 1540
  321.5 142.6 %copy-start.117 = (s32[25]{0:T(128)S(1)}, s32[25]{0:T(128)}, u32[]{:S(2)}) copy-start(s32[25]{0:T(128)} %param.8) | copy-start | bytes 304
  (107 other events, 1198.5 us)
where the time goes:
time: 470 us; the launch traced here: 467 us
  starting transfers between devices  115 us (24%)
  other arithmetic  114 us (24%)
  blocking collectives  98.9 us (21%)
  matrix products  61.7 us (13%)
  local copies, waits for them, and re-layouts  56.2 us (12%)
  between operations  11 us (2%)
  waiting for transfers between devices  10.4 us (2%)
    psum x1, blocking collectives, body(): lax.psum((partial_grad, log_sum, log_first), ('wide', 'grp'))  98.9 us
    ppermute x15, starting transfers between devices, partner_2(): return lax.ppermute(value, axis, pairs)  68.5 us
    all_to_all x4, starting transfers between devices, regroup(): lax.all_to_all(three_way, 'grp', split_axis=0, concat_axis=0, tiled=True)  29.7 us
    add x4, other arithmetic, rate_of(): offsets[position] + by_row[:, position][:, None]  21.3 us
    dot_general x25, matrix products, feature_row(): return jnp.dot(listed, to_global, precision=highest) + whole * own_column  20.8 us
    another operation x26, local copies, waits for them, and re-layouts, join_rows(): paired = jnp.stack([lower_half, upper_half], axis=1)  20.4 us
    mul x13, other arithmetic, local_pull(): rates[:, 0] * others[:, 1]  18.7 us
    mul x2, other arithmetic, feature_row(): whole * device_values  15.8 us
  transfers between devices with their start and end apart: 21, of which 2 were waited for; matrix products, arithmetic and copies ran while one was open for 31% of the time, Pallas kernels for 0%

commit v1 on v0

--- a/solution.py
+++ b/solution.py
@@ -300,7 +300,7 @@
         )
     partial_grad = jnp.stack(grad_rows)
     grad_total, log_total, empty_state = lax.psum(
-        (partial_grad, log_sum, log_first), ("wide", "grp")
+        lax.psum((partial_grad, log_sum, log_first), axis_name="wide"), axis_name="grp"
     )
     gradient = jnp.dot(onehot, jnp.dot(grad_total, onehot.T, precision=highest), precision=highest)
     loglik = log_total / patient_count

time: 470 us -> 554 us (1.18)
  blocking collectives: 98.9 us -> 179 us
    psum x1 -> x2, blocking collectives: 98.9 us -> 179 us  [the longest x1 91.5 us: body(): lax.psum((partial_grad, log_sum, log_first), axis_name='wide')]
  transfers between devices with their start and end apart: 21 -> 21, of which waited for: 2 -> 2; matrix products, arithmetic and copies ran while one was open for 31% -> 27% of each run, Pallas kernels for 0% -> 0%
where the time goes in v1:
time: 554 us; the launch traced here: 547 us
  blocking collectives  179 us (32%)
  starting transfers between devices  115 us (21%)
  other arithmetic  114 us (21%)
  matrix products  61.7 us (11%)
  local copies, waits for them, and re-layouts  56.2 us (10%)
  between operations  11 us (2%)
  waiting for transfers between devices  10.4 us (2%)
    psum x1, blocking collectives, body(): lax.psum((partial_grad, log_sum, log_first), axis_name='wide')  91.5 us
    psum x1, blocking collectives, body(): lax.psum(lax.psum((partial_grad, log_sum, log_first), axis_name='wide'),...  87.8 us
    ppermute x15, starting transfers between devices, partner_2(): return lax.ppermute(value, axis, pairs)  68.5 us
    all_to_all x4, starting transfers between devices, regroup(): lax.all_to_all(three_way, 'grp', split_axis=0, concat_axis=0, tiled=True)  29.7 us
    add x4, other arithmetic, rate_of(): offsets[position] + by_row[:, position][:, None]  21.3 us
    dot_general x25, matrix products, feature_row(): return jnp.dot(listed, to_global, precision=highest) + whole * own_column  20.8 us
    another operation x26, local copies, waits for them, and re-layouts, join_rows(): paired = jnp.stack([lower_half, upper_half], axis=1)  20.4 us
    mul x13, other arithmetic, local_pull(): rates[:, 0] * others[:, 1]  18.7 us
  transfers between devices with their start and end apart: 21, of which 2 were waited for; matrix products, arithmetic and copies ran while one was open for 27% of the time, Pallas kernels for 0%

profile of v1, /device:TPU:1, one launch (start us, length us, event | category | flops | bytes accessed | tf_op | source)
XLA Modules:
  0.0 547.2 jit_solution(6981198604250414685)
XLA Ops:
  7.5 6.0 %fusion.490 = (f32[512]{0:T(512)S(1)}, f32[512,1]{0,1:T(1,128)}, f32[512,1]{0,1:T(1,128)S(1)}, f32[512,1]{0,1:T(1,128)S(1)}, f32[512,1]{0,1:T(1,128)S(1)}, /*ind...) fusion(f32[]{:T(128)} %broadcast.1002, f32[512,25]{0,1:T(8,128)S(1)} %fusion.133, ...), kind=kLoop, calls=%fused_computation.907 | loop fusion | flops 4096 | bytes 34852 | tf_op jit(solution)/shard_map/add | solution.py:65
  20.2 6.1 %slice_add_fusion.3 = (f32[512,1]{0,1:T(1,128)}, f32[512,1]{0,1:T(1,128)}, f32[512,1]{0,1:T(1,128)}, f32[512,1]{0,1:T(1,128)}, f32[512,1]{0,1:T(1,128)S(1)}, /*i...) fusion(f32[512,25]{0,1:T(8,128)S(1)} %fusion.133, f32[]{:T(128)} %bitcast.119, ...), kind=kLoop, calls=%fused_computation.517 | loop fusion | flops 4608 | bytes 36900 | tf_op jit(solution)/shard_map/add | solution.py:65
  26.5 2.5 fusion.100
  29.1 4.4 collective-permute-start
  33.4 4.9 collective-permute-start.1
  38.3 8.8 %collective-permute-start.2 = (f32[512,128]{1,0:T(8,128)}, f32[512,128]{1,0:T(8,128)}, u32[]{:S(2)}, u32[]{:S(2)}) collective-permute-start(f32[512,128]{1,0:T(8,128)} %get-tuple-element.147), channel_id=1, source_target_pairs={{0,64},{16,80},{32,96},{48,112},{64,0},{80,16},{96,32},{112,48},{1... | collective-permute-start | bytes 786440 | tf_op jit(solution)/shard_map/ppermute | solution.py:13
  47.2 7.9 %collective-permute-start.3 = (f32[512,128]{1,0:T(8,128)}, f32[512,128]{1,0:T(8,128)}, u32[]{:S(2)}, u32[]{:S(2)}) collective-permute-start(f32[512,128]{1,0:T(8,128)} %get-tuple-element.148), channel_id=1, source_target_pairs={{0,128},{16,144},{32,160},{48,176},{64,192},{80,208},{96,224},{112... | collective-permute-start | bytes 786440 | tf_op jit(solution)/shard_map/ppermute | solution.py:13
  55.1 3.1 collective-permute-start.4
  59.1 8.7 %all-to-all-start.2 = ((f32[16,32,128]{2,1,0:T(8,128)}), f32[16,32,128]{2,1,0:T(8,128)S(1)}, u32[]{:S(2)}, u32[]{:S(2)}) async-start(f32[16,32,128]{2,1,0:T(8,128)} %bitcast.160), calls=%async_computation.2 | async-start | bytes 524288 | tf_op jit(solution)/shard_map/all_to_all | solution.py:203
  71.5 3.1 fusion.264
  77.0 6.2 %fusion.483 = (f32[512]{0:T(512)S(1)}, f32[512,1]{0,1:T(1,128)}, f32[512,1]{0,1:T(1,128)}, f32[512]{0:T(512)S(1)}, f32[512,1]{0,1:T(1,128)}, /*index=5*/f32[512]...) fusion(f32[]{:T(128)} %broadcast.1002, ...), kind=kLoop, calls=%fused_computation.900 | loop fusion | flops 4096 | bytes 47140 | tf_op jit(solution)/shard_map/add | solution.py:65
  96.2 1.8 slice_multiply_fusion.25
  98.0 1.8 slice_multiply_fusion.31
  106.6 1.7 slice_multiply_fusion.30
  110.6 7.2 %all-to-all-start = ((f32[16,32,128]{2,1,0:T(8,128)}), f32[16,32,128]{2,1,0:T(8,128)S(1)}, u32[]{:S(2)}, u32[]{:S(2)}) async-start(f32[16,32,128]{2,1,0:T(8,128)} %bitcast.66), calls=%async_computation | async-start | bytes 524288 | tf_op jit(solution)/shard_map/all_to_all | solution.py:203
  117.8 2.1 slice_multiply_fusion.32
  119.9 6.6 %all-to-all-done = f32[16,32,128]{2,1,0:T(8,128)S(1)} async-done(((f32[16,32,128]{2,1,0:T(8,128)}), f32[16,32,128]{2,1,0:T(8,128)S(1)}, u32[]{:S(2)}, u32[]{:S(2)}) %all-to-all-start) | async-done | bytes 262176 | tf_op jit(solution)/shard_map/all_to_all | solution.py:203
  130.1 4.8 all-to-all-start.3
  138.7 2.6 collective-permute-start.5
  141.3 3.1 collective-permute-start.6
  144.4 5.2 collective-permute-start.7
  149.6 1.9 collective-permute-start.8
  151.6 1.9 collective-permute-start.9
  153.5 9.0 %all-to-all-start.1 = ((f32[16,32,128]{2,1,0:T(8,128)}), f32[16,32,128]{2,1,0:T(8,128)}, u32[]{:S(2)}, u32[]{:S(2)}) async-start(f32[16,32,128]{2,1,0:T(8,128)} %fusion.93), calls=%async_computation.1 | async-start | bytes 524288 | tf_op jit(solution)/shard_map/all_to_all | solution.py:203
  164.4 1.7 stack.270
  167.0 1.8 stack.248
  200.4 2.7 scatter_custom_fusion
  204.8 10.6 %fusion.84 = (f32[512,128]{1,0:T(8,128)}, f32[512,128]{1,0:T(8,128)}) fusion(f32[512,128]{1,0:T(8,128)} %bitcast.870, f32[512,128]{1,0:T(8,128)} %bitcast.863, f32[512,128]{1,0:T(8,128)} %bitcast.862, f32[512,896]{1,0:T(8,128)S(1)} %fusion.414, f32[16,32,128]{2,1,0:T(8,128)} %all-to-all-done.3, f32[1,2,256,128]{3,2,1,0:T(8,128)} %stack.278, ...), kind=kOutput, calls=%fused_computation.214 | convolution fusion | flops 713555968 | bytes 12508344 | tf_op jit(solution)/shard_map/dot_general | solution.py:87
  215.5 3.2 collective-permute-start.11
  218.7 7.5 %collective-permute-start.12 = (f32[512,128]{1,0:T(8,128)}, f32[512,128]{1,0:T(8,128)}, u32[]{:S(2)}, u32[]{:S(2)}) collective-permute-start(f32[512,128]{1,0:T(8,128)} %get-tuple-element.287), channel_id=1, source_target_pairs={{0,64},{16,80},{32,96},{48,112},{64,0},{80,16},{96,32},{112,48},{1... | collective-permute-start | bytes 786440 | tf_op jit(solution)/shard_map/ppermute | solution.py:13
  226.3 8.8 %collective-permute-start.13 = (f32[512,128]{1,0:T(8,128)}, f32[512,128]{1,0:T(8,128)}, u32[]{:S(2)}, u32[]{:S(2)}) collective-permute-start(f32[512,128]{1,0:T(8,128)} %get-tuple-element.287), channel_id=1, source_target_pairs={{0,128},{16,144},{32,160},{48,176},{64,192},{80,208},{96,224},{112... | collective-permute-start | bytes 786440 | tf_op jit(solution)/shard_map/ppermute | solution.py:13
  235.1 2.2 collective-permute-start.14
  237.3 1.9 fusion.498
  239.2 2.8 collective-permute-start.10
  252.1 9.2 %all-to-all-start.4 = ((f32[16,32,128]{2,1,0:T(8,128)}), f32[16,32,128]{2,1,0:T(8,128)S(1)}, u32[]{:S(2)}, u32[]{:S(2)}) async-start(f32[16,32,128]{2,1,0:T(8,128)} %bitcast.293), calls=%async_computation.4 | async-start | bytes 524288 | tf_op jit(solution)/shard_map/all_to_all | solution.py:273
  261.4 2.4 fusion.54
  277.9 1.9 fusion.477
  283.1 1.8 fusion.141
  285.6 2.9 gather_fusion.1
  290.2 7.2 %all-to-all-start.5 = ((f32[16,32,128]{2,1,0:T(8,128)}), f32[16,32,128]{2,1,0:T(8,128)S(1)}, u32[]{:S(2)}, u32[]{:S(2)}) async-start(f32[16,32,128]{2,1,0:T(8,128)} %bitcast.295), calls=%async_computation.5 | async-start | bytes 524288 | tf_op jit(solution)/shard_map/all_to_all | solution.py:274
  300.6 1.8 fusion.139
  302.4 3.7 all-to-all-done.5
  306.1 1.8 pad_reduce_fusion.2
  326.6 11.2 %broadcast_multiply_fusion.1 = (f32[9]{0:T(128)S(1)}, f32[9]{0:T(128)S(1)}, f32[9]{0:T(128)S(1)}, f32[9]{0:T(128)S(1)}, f32[9]{0:T(128)S(1)}, /*index=5*/f32[9]{...) fusion(f32[]{:T(128)} %get-tuple-element.5, ...), kind=kLoop, calls=%fused_computation.779 | loop fusion | flops 171 | bytes 756 | tf_op jit(solution)/shard_map/mul | solution.py:143
  352.8 4.5 broadcast_multiply_fusion.19
  363.3 1.8 fusion.52
  365.1 91.5 %all-reduce.39 = (f32[]{:T(128)}, f32[25,25]{1,0:T(8,128)S(1)}, f32[]{:T(128)}) all-reduce(f32[]{:T(128)} %select_reduce_fusion, f32[25,25]{1,0:T(8,128)S(1)} %stack.321, f32[]{:T(128)S(6)} %select_n.72), channel_id=1, replica_groups=mesh['wide'=32,'grp'=16] {'wide'}, use_global_device_ids=true, to_apply=%region_2.3 | all-reduce | flops 627 | bytes 5016 | tf_op jit(solution)/shard_map/psum | solution.py:303
  456.6 87.8 %all-reduce.40 = (f32[]{:T(128)}, f32[25,25]{1,0:T(8,128)S(1)}, f32[]{:T(128)}) all-reduce(f32[]{:T(128)} %get-tuple-element.82, f32[25,25]{1,0:T(8,128)S(1)} %get-tuple-element.83, f32[]{:T(128)} %get-tuple-element.84), channel_id=1, replica_groups=mesh['wide'=32,'grp'=16] {'grp'}, use_global_device_ids=true, to_apply=%region_3.4 | all-reduce | flops 627 | bytes 5016 | tf_op jit(solution)/shard_map/psum | solution.py:302
  (543 shorter events, 151.9 us)
Async XLA Ops:
  0.7 69.5 %copy-start.43 = (f32[5]{0:T(128)}, f32[5]{0:T(128)S(1)}, u32[]{:S(2)}) copy-start(f32[5]{0:T(128)S(1)} %and_convert_fusion) | copy-start | bytes 64
  1.4 68.9 %copy-start.46 = (f32[4]{0:T(128)}, f32[4]{0:T(128)S(1)}, u32[]{:S(2)}) copy-start(f32[4]{0:T(128)S(1)} %and_convert_fusion.1) | copy-start | bytes 52
  16.9 41.4 %copy-start.2 = (f32[65536]{0:T(1024)S(1)}, f32[65536]{0:T(1024)}, u32[]{:S(2)}) copy-start(f32[65536]{0:T(1024)} %param.11) | copy-start | bytes 786436
  26.4 57.0 %copy-start.62 = (f32[512,1]{0,1:T(1,128)}, f32[512,1]{0,1:T(1,128)S(1)}, u32[]{:S(2)}) copy-start(f32[512,1]{0,1:T(1,128)S(1)} %get-tuple-element.158) | copy-start | bytes 6148
  26.4 57.0 %copy-start.64 = (f32[512,1]{0,1:T(1,128)}, f32[512,1]{0,1:T(1,128)S(1)}, u32[]{:S(2)}) copy-start(f32[512,1]{0,1:T(1,128)S(1)} %get-tuple-element.154) | copy-start | bytes 6148
  26.4 57.0 %copy-start.66 = (f32[512,1]{0,1:T(1,128)}, f32[512,1]{0,1:T(1,128)S(1)}, u32[]{:S(2)}) copy-start(f32[512,1]{0,1:T(1,128)S(1)} %get-tuple-element.155) | copy-start | bytes 6148
  26.4 57.0 %copy-start.68 = (f32[512,1]{0,1:T(1,128)}, f32[512,1]{0,1:T(1,128)S(1)}, u32[]{:S(2)}) copy-start(f32[512,1]{0,1:T(1,128)S(1)} %get-tuple-element.156) | copy-start | bytes 6148
  26.4 57.0 %copy-start.70 = (f32[512,1]{0,1:T(1,128)}, f32[512,1]{0,1:T(1,128)S(1)}, u32[]{:S(2)}) copy-start(f32[512,1]{0,1:T(1,128)S(1)} %get-tuple-element.157) | copy-start | bytes 6148
  26.4 60.7 %copy-start.115 = (s32[256]{0:T(256)S(1)}, s32[256]{0:T(256)}, u32[]{:S(2)}) copy-start(s32[256]{0:T(256)} %param.9) | copy-start | bytes 3076
  26.4 60.7 %copy-start.116 = (s32[25]{0:T(128)S(1)}, s32[25]{0:T(128)}, u32[]{:S(2)}) copy-start(s32[25]{0:T(128)} %param.8) | copy-start | bytes 304
  29.0 59.5 %copy-start.40 = (f32[512,896]{1,0:T(8,128)}, f32[512,896]{1,0:T(8,128)S(1)}, u32[]{:S(2)}) copy-start(f32[512,896]{1,0:T(8,128)S(1)} %get-tuple-element.144) | copy-start | bytes 5505028
  29.1 109.6 %collective-permute-start = (f32[512,128]{1,0:T(8,128)}, f32[512,128]{1,0:T(8,128)}, u32[]{:S(2)}, u32[]{:S(2)}) collective-permute-start(f32[512,128]{1,0:T(8,128)} %get-tuple-element.145), channel_id=1, source_target_pairs={{0,16},{16,0},{32,48},{48,32},{64,80},{80,64},{96,112},{112,96},{1... | collective-permute-start | bytes 786440 | tf_op jit(solution)/shard_map/ppermute | solution.py:13
  33.4 107.9 %collective-permute-start.1 = (f32[512,128]{1,0:T(8,128)}, f32[512,128]{1,0:T(8,128)}, u32[]{:S(2)}, u32[]{:S(2)}) collective-permute-start(f32[512,128]{1,0:T(8,128)} %get-tuple-element.146), channel_id=1, source_target_pairs={{0,32},{16,48},{32,0},{48,16},{64,96},{80,112},{96,64},{112,80},{1... | collective-permute-start | bytes 786440 | tf_op jit(solution)/shard_map/ppermute | solution.py:13
  38.3 106.1 %collective-permute-start.2 = (f32[512,128]{1,0:T(8,128)}, f32[512,128]{1,0:T(8,128)}, u32[]{:S(2)}, u32[]{:S(2)}) collective-permute-start(f32[512,128]{1,0:T(8,128)} %get-tuple-element.147), channel_id=1, source_target_pairs={{0,64},{16,80},{32,96},{48,112},{64,0},{80,16},{96,32},{112,48},{1... | collective-permute-start | bytes 786440 | tf_op jit(solution)/shard_map/ppermute | solution.py:13
  47.2 102.5 %collective-permute-start.3 = (f32[512,128]{1,0:T(8,128)}, f32[512,128]{1,0:T(8,128)}, u32[]{:S(2)}, u32[]{:S(2)}) collective-permute-start(f32[512,128]{1,0:T(8,128)} %get-tuple-element.148), channel_id=1, source_target_pairs={{0,128},{16,144},{32,160},{48,176},{64,192},{80,208},{96,224},{112... | collective-permute-start | bytes 786440 | tf_op jit(solution)/shard_map/ppermute | solution.py:13
  55.1 96.5 %collective-permute-start.4 = (f32[512,128]{1,0:T(8,128)}, f32[512,128]{1,0:T(8,128)}, u32[]{:S(2)}, u32[]{:S(2)}) collective-permute-start(f32[512,128]{1,0:T(8,128)} %get-tuple-element.149), channel_id=1, source_target_pairs={{0,256},{16,272},{32,288},{48,304},{64,320},{80,336},{96,352},{112... | collective-permute-start | bytes 786440 | tf_op jit(solution)/shard_map/ppermute | solution.py:13
  59.1 51.5 %all-to-all-start.2 = ((f32[16,32,128]{2,1,0:T(8,128)}), f32[16,32,128]{2,1,0:T(8,128)S(1)}, u32[]{:S(2)}, u32[]{:S(2)}) async-start(f32[16,32,128]{2,1,0:T(8,128)} %bitcast.160), calls=%async_computation.2 | async-start | bytes 524288 | tf_op jit(solution)/shard_map/all_to_all | solution.py:203
  110.6 15.9 %all-to-all-start = ((f32[16,32,128]{2,1,0:T(8,128)}), f32[16,32,128]{2,1,0:T(8,128)S(1)}, u32[]{:S(2)}, u32[]{:S(2)}) async-start(f32[16,32,128]{2,1,0:T(8,128)} %bitcast.66), calls=%async_computation | async-start | bytes 524288 | tf_op jit(solution)/shard_map/all_to_all | solution.py:203
  130.1 23.4 %all-to-all-start.3 = ((f32[16,32,128]{2,1,0:T(8,128)}), f32[16,32,128]{2,1,0:T(8,128)}, u32[]{:S(2)}, u32[]{:S(2)}) async-start(f32[16,32,128]{2,1,0:T(8,128)} %fusion.91), calls=%async_computation.3 | async-start | bytes 524288 | tf_op jit(solution)/shard_map/all_to_all | solution.py:203
  136.9 29.3 %copy-start.30 = (f32[128,1,2,128]{3,2,1,0:T(2,128)S(1)}, f32[128,1,2,128]{3,2,1,0:T(2,128)}, u32[]{:S(2)}) copy-start(f32[128,1,2,128]{3,2,1,0:T(2,128)} %get-tuple-element.140) | copy-start | bytes 393220
  137.9 30.8 %copy-start.29 = (f32[128,1,2,128]{3,2,1,0:T(2,128)S(1)}, f32[128,1,2,128]{3,2,1,0:T(2,128)}, u32[]{:S(2)}) copy-start(f32[128,1,2,128]{3,2,1,0:T(2,128)} %get-tuple-element.141) | copy-start | bytes 393220
  138.7 66.0 %collective-permute-start.5 = (f32[512,128]{1,0:T(8,128)}, f32[512,128]{1,0:T(8,128)}, u32[]{:S(2)}, u32[]{:S(2)}) collective-permute-start(f32[512,128]{1,0:T(8,128)} %get-tuple-element.116), channel_id=1, source_target_pairs={{0,16},{16,0},{32,48},{48,32},{64,80},{80,64},{96,112},{112,96},{1... | collective-permute-start | bytes 786440 | tf_op jit(solution)/shard_map/ppermute | solution.py:13
  141.3 63.4 %collective-permute-start.6 = (f32[512,128]{1,0:T(8,128)}, f32[512,128]{1,0:T(8,128)}, u32[]{:S(2)}, u32[]{:S(2)}) collective-permute-start(f32[512,128]{1,0:T(8,128)} %get-tuple-element.116), channel_id=1, source_target_pairs={{0,32},{16,48},{32,0},{48,16},{64,96},{80,112},{96,64},{112,80},{1... | collective-permute-start | bytes 786440 | tf_op jit(solution)/shard_map/ppermute | solution.py:13
  144.4 60.3 %collective-permute-start.7 = (f32[512,128]{1,0:T(8,128)}, f32[512,128]{1,0:T(8,128)}, u32[]{:S(2)}, u32[]{:S(2)}) collective-permute-start(f32[512,128]{1,0:T(8,128)} %get-tuple-element.116), channel_id=1, source_target_pairs={{0,64},{16,80},{32,96},{48,112},{64,0},{80,16},{96,32},{112,48},{1... | collective-permute-start | bytes 786440 | tf_op jit(solution)/shard_map/ppermute | solution.py:13
  149.6 55.1 %collective-permute-start.8 = (f32[512,128]{1,0:T(8,128)}, f32[512,128]{1,0:T(8,128)}, u32[]{:S(2)}, u32[]{:S(2)}) collective-permute-start(f32[512,128]{1,0:T(8,128)} %get-tuple-element.116), channel_id=1, source_target_pairs={{0,128},{16,144},{32,160},{48,176},{64,192},{80,208},{96,224},{112... | collective-permute-start | bytes 786440 | tf_op jit(solution)/shard_map/ppermute | solution.py:13
  151.6 53.2 %collective-permute-start.9 = (f32[512,128]{1,0:T(8,128)}, f32[512,128]{1,0:T(8,128)}, u32[]{:S(2)}, u32[]{:S(2)}) collective-permute-start(f32[512,128]{1,0:T(8,128)} %get-tuple-element.116), channel_id=1, source_target_pairs={{0,256},{16,272},{32,288},{48,304},{64,320},{80,336},{96,352},{112... | collective-permute-start | bytes 786440 | tf_op jit(solution)/shard_map/ppermute | solution.py:13
  153.5 51.3 %all-to-all-start.1 = ((f32[16,32,128]{2,1,0:T(8,128)}), f32[16,32,128]{2,1,0:T(8,128)}, u32[]{:S(2)}, u32[]{:S(2)}) async-start(f32[16,32,128]{2,1,0:T(8,128)} %fusion.93), calls=%async_computation.1 | async-start | bytes 524288 | tf_op jit(solution)/shard_map/all_to_all | solution.py:203
  215.5 28.9 %copy-start.16 = (f32[128,2,2,128]{3,2,1,0:T(2,128)S(1)}, f32[128,2,2,128]{3,2,1,0:T(2,128)}, u32[]{:S(2)}) copy-start(f32[128,2,2,128]{3,2,1,0:T(2,128)} %copy-done.15) | copy-start | bytes 786436
  215.5 99.1 %collective-permute-start.11 = (f32[512,128]{1,0:T(8,128)}, f32[512,128]{1,0:T(8,128)}, u32[]{:S(2)}, u32[]{:S(2)}) collective-permute-start(f32[512,128]{1,0:T(8,128)} %get-tuple-element.287), channel_id=1, source_target_pairs={{0,32},{16,48},{32,0},{48,16},{64,96},{80,112},{96,64},{112,80},{1... | collective-permute-start | bytes 786440 | tf_op jit(solution)/shard_map/ppermute | solution.py:13
  218.7 95.8 %collective-permute-start.12 = (f32[512,128]{1,0:T(8,128)}, f32[512,128]{1,0:T(8,128)}, u32[]{:S(2)}, u32[]{:S(2)}) collective-permute-start(f32[512,128]{1,0:T(8,128)} %get-tuple-element.287), channel_id=1, source_target_pairs={{0,64},{16,80},{32,96},{48,112},{64,0},{80,16},{96,32},{112,48},{1... | collective-permute-start | bytes 786440 | tf_op jit(solution)/shard_map/ppermute | solution.py:13
  226.3 88.3 %collective-permute-start.13 = (f32[512,128]{1,0:T(8,128)}, f32[512,128]{1,0:T(8,128)}, u32[]{:S(2)}, u32[]{:S(2)}) collective-permute-start(f32[512,128]{1,0:T(8,128)} %get-tuple-element.287), channel_id=1, source_target_pairs={{0,128},{16,144},{32,160},{48,176},{64,192},{80,208},{96,224},{112... | collective-permute-start | bytes 786440 | tf_op jit(solution)/shard_map/ppermute | solution.py:13
  235.1 79.5 %collective-permute-start.14 = (f32[512,128]{1,0:T(8,128)}, f32[512,128]{1,0:T(8,128)}, u32[]{:S(2)}, u32[]{:S(2)}) collective-permute-start(f32[512,128]{1,0:T(8,128)} %get-tuple-element.287), channel_id=1, source_target_pairs={{0,256},{16,272},{32,288},{48,304},{64,320},{80,336},{96,352},{112... | collective-permute-start | bytes 786440 | tf_op jit(solution)/shard_map/ppermute | solution.py:13
  239.2 80.5 %collective-permute-start.10 = (f32[512,128]{1,0:T(8,128)}, f32[512,128]{1,0:T(8,128)}, u32[]{:S(2)}, u32[]{:S(2)}) collective-permute-start(f32[512,128]{1,0:T(8,128)} %get-tuple-element.287), channel_id=1, source_target_pairs={{0,16},{16,0},{32,48},{48,32},{64,80},{80,64},{96,112},{112,96},{1... | collective-permute-start | bytes 786440 | tf_op jit(solution)/shard_map/ppermute | solution.py:13
  252.1 38.1 %all-to-all-start.4 = ((f32[16,32,128]{2,1,0:T(8,128)}), f32[16,32,128]{2,1,0:T(8,128)S(1)}, u32[]{:S(2)}, u32[]{:S(2)}) async-start(f32[16,32,128]{2,1,0:T(8,128)} %bitcast.293), calls=%async_computation.4 | async-start | bytes 524288 | tf_op jit(solution)/shard_map/all_to_all | solution.py:273
  290.2 15.9 %all-to-all-start.5 = ((f32[16,32,128]{2,1,0:T(8,128)}), f32[16,32,128]{2,1,0:T(8,128)S(1)}, u32[]{:S(2)}, u32[]{:S(2)}) async-start(f32[16,32,128]{2,1,0:T(8,128)} %bitcast.295), calls=%async_computation.5 | async-start | bytes 524288 | tf_op jit(solution)/shard_map/all_to_all | solution.py:274
  321.4 28.8 %copy-start.126 = (f32[9]{0:T(128)S(1)}, f32[9]{0:T(128)}, u32[]{:S(2)}) copy-start(f32[9]{0:T(128)} %convolution_bitcast_fusion.15) | copy-start | bytes 112
  321.4 28.8 %copy-start.127 = (f32[7]{0:T(128)S(1)}, f32[7]{0:T(128)}, u32[]{:S(2)}) copy-start(f32[7]{0:T(128)} %convolution_bitcast_fusion.56) | copy-start | bytes 88
  321.4 29.6 %copy-start.128 = (f32[9]{0:T(128)S(1)}, f32[9]{0:T(128)}, u32[]{:S(2)}) copy-start(f32[9]{0:T(128)} %convolution_bitcast_fusion.16) | copy-start | bytes 112
  321.4 29.6 %copy-start.130 = (f32[7]{0:T(128)S(1)}, f32[7]{0:T(128)}, u32[]{:S(2)}) copy-start(f32[7]{0:T(128)} %convolution_bitcast_fusion.58) | copy-start | bytes 88
  321.4 30.5 %copy-start.129 = (f32[9]{0:T(128)S(1)}, f32[9]{0:T(128)}, u32[]{:S(2)}) copy-start(f32[9]{0:T(128)} %convolution_bitcast_fusion.17) | copy-start | bytes 112
  321.4 30.5 %copy-start.131 = (f32[7]{0:T(128)S(1)}, f32[7]{0:T(128)}, u32[]{:S(2)}) copy-start(f32[7]{0:T(128)} %convolution_bitcast_fusion.60) | copy-start | bytes 88
  321.4 36.7 %copy-start.119 = (f32[9]{0:T(128)S(1)}, f32[9]{0:T(128)}, u32[]{:S(2)}) copy-start(f32[9]{0:T(128)} %convolution_bitcast_fusion.19) | copy-start | bytes 112
  321.5 36.7 %copy-start.120 = (f32[7]{0:T(128)S(1)}, f32[7]{0:T(128)}, u32[]{:S(2)}) copy-start(f32[7]{0:T(128)} %convolution_bitcast_fusion.64) | copy-start | bytes 88
  321.5 37.5 %copy-start.118 = (f32[9]{0:T(128)S(1)}, f32[9]{0:T(128)}, u32[]{:S(2)}) copy-start(f32[9]{0:T(128)} %convolution_bitcast_fusion.20) | copy-start | bytes 112
  321.5 37.5 %copy-start.121 = (f32[7]{0:T(128)S(1)}, f32[7]{0:T(128)}, u32[]{:S(2)}) copy-start(f32[7]{0:T(128)} %convolution_bitcast_fusion.66) | copy-start | bytes 88
  321.5 41.8 %copy-start.132 = (pred[128]{0:T(512)(128)(4,1)S(1)}, pred[128]{0:T(512)(128)(4,1)}, u32[]{:S(2)}) copy-start(pred[128]{0:T(512)(128)(4,1)} %iota_compare_fusion.12) | copy-start | bytes 388
  321.5 41.8 %copy-start.133 = (pred[512]{0:T(512)(128)(4,1)S(1)}, pred[512]{0:T(512)(128)(4,1)}, u32[]{:S(2)}) copy-start(pred[512]{0:T(512)(128)(4,1)} %fusion.269) | copy-start | bytes 1540
  321.5 222.9 %copy-start.117 = (s32[25]{0:T(128)S(1)}, s32[25]{0:T(128)}, u32[]{:S(2)}) copy-start(s32[25]{0:T(128)} %param.8) | copy-start | bytes 304
  (107 other events, 1198.5 us)
